TPU v7x, 32 devices: a whole 2x2x4 slice. The times are simulated.
32 devices in a mesh: pipe: 4 (over y, x), ctx: 2 (over core), tp: 4 (over z).
Axes of the slice: x: 2, y: 2, z: 4, core: 2. Of those that a mesh axis runs over, the one named last changes fastest.
Arguments:
- fwd_acts: bfloat16 [4, 256, 16384], P('pipe', 'ctx', 'tp'), may hold values from -6 to 6
- back_grads: bfloat16 [4, 256, 16384], P('pipe', 'ctx', 'tp'), may hold values from -6 to 6
- stashed: bfloat16 [4, 3, 256, 16384], P('pipe', None, 'ctx', 'tp'), may hold values from -6 to 6
- layer_weights: bfloat16 [2, 4, 16384, 2304], P(None, 'pipe', 'tp', 'ctx')
- span_order: int32 [8], replicated, may hold values from 0 to 7, each once
- fwd_docs: int32 [4, 256], replicated, may hold values from 0 to 3, never falling along the last dimension, each value on 1 to 128 neighbouring positions
- back_docs: int32 [4, 256], replicated, may hold values from 0 to 3, never falling along the last dimension, each value on 1 to 128 neighbouring positions
Outputs:
- fwd_out: bfloat16 [4, 256, 16384], P('pipe', 'ctx', 'tp')
- back_out: bfloat16 [4, 256, 16384], P('pipe', 'ctx', 'tp')
Inputs may be any that keep to these rules, and one draw needn't show every extreme that they name: Each span number appears once; device i of ctx stores spans span_order[4 * i] to span_order[4 i + 3]. `fwd_docs`: ids never fall along positions; each document covers 1 to 128 positions, one exactly 128. `back_docs`: ids never fall along positions; each document covers 1 to 128 positions, one exactly 128.
All inputs are finite; a program needn't handle non-finite values.
Results may differ from a plain program's by a relative error of at most 0.014.
The roundings to bfloat16 on the way count: a program that leaves them out, or rounds other values in their place, can miss the bound.
Values may be sent and summed in bfloat16 or wider, within the bound.
A program may use at most 384 MiB of HBM per device.

v0:
```python
import jax
import jax.numpy as jnp
from jax import lax
from jax.sharding import PartitionSpec as P

HD = 128
QH = 8
SPANS = 4


EPSILON = 1e-05


def from_behind(block, axis, distance):
    devices = range(lax.axis_size(axis))
    route = [((i - distance) % len(devices), i) for i in devices]
    return lax.ppermute(block, axis, route)


def visible(query_pos, query_doc, key_pos, key_doc):
    return (key_pos[None, :] <= query_pos[:, None]) & (key_doc[None, :] == query_doc[:, None])


def softmax_rows(scores, visible_mask):
    masked = jnp.where(visible_mask, scores, -jnp.inf)
    row_max = jnp.max(masked, axis=-1, keepdims=True)
    exponent = jnp.where(visible_mask, jnp.exp(masked - row_max), 0.0)
    return exponent / jnp.sum(exponent, axis=-1, keepdims=True)


def seq_documents(docs_table, slot_index, span_order, span_len):
    docs_row = lax.dynamic_index_in_dim(docs_table, slot_index, 0, keepdims=False)
    return docs_row.reshape(-1, span_len)[span_order].reshape(-1)


def forward_layer(hidden, weight, positions, documents, ctx_rank, model_width):
    row_count = hidden.shape[0]
    qkv_cols = QH * HD + 2 * HD
    score_scale = HD ** (-0.5)
    hidden_f = hidden.astype(jnp.float32)
    partial_m = jnp.dot(hidden, weight[:, :qkv_cols], preferred_element_type=jnp.float32)
    partial_sq = jnp.sum(hidden_f * hidden_f, axis=1)
    merged, squares = lax.psum((partial_m, partial_sq), "tp")
    inv_rms = lax.rsqrt(squares / model_width + EPSILON)
    qkv = (inv_rms[:, None] * merged).astype(jnp.bfloat16)
    queries = qkv[:, : QH * HD].reshape(row_count, QH, HD)
    keys_own = qkv[:, QH * HD : QH * HD + HD]
    values_own = qkv[:, QH * HD + HD : qkv_cols]
    keys_all, values_all = (
        lax.all_gather(keys_own, "ctx", axis=0, tiled=True),
        lax.all_gather(values_own, "ctx", axis=0, tiled=True),
    )
    own_pos = lax.dynamic_slice_in_dim(positions, ctx_rank * row_count, row_count)
    own_doc = lax.dynamic_slice_in_dim(documents, ctx_rank * row_count, row_count)
    visible_mask = visible(own_pos, own_doc, positions, documents)
    scores = (
        jnp.einsum("qhc,kc->hqk", queries, keys_all, preferred_element_type=jnp.float32)
        * score_scale
    )
    attn_probs = softmax_rows(scores, visible_mask[None]).astype(jnp.bfloat16)
    attended = jnp.einsum("hqk,kc->qhc", attn_probs, values_all, preferred_element_type=jnp.float32)
    attended = attended.reshape(row_count, QH * HD).astype(jnp.bfloat16)
    update = jnp.einsum(
        "rc,dc->rd", attended, weight[:, qkv_cols:], preferred_element_type=jnp.float32
    )
    return (hidden_f + update).astype(jnp.bfloat16)


def backward_layer(stash_point, incoming, weight, positions, documents, ctx_rank, model_width):
    row_count = stash_point.shape[0]
    qkv_cols = QH * HD + 2 * HD
    score_scale = HD ** (-0.5)
    stash_f = stash_point.astype(jnp.float32)
    partial_m = jnp.dot(stash_point, weight[:, :qkv_cols], preferred_element_type=jnp.float32)
    partial_sq = jnp.sum(stash_f * stash_f, axis=1)
    partial_out = jnp.dot(incoming, weight[:, qkv_cols:], preferred_element_type=jnp.float32)
    merged, squares, out_sum = lax.psum((partial_m, partial_sq, partial_out), "tp")
    inv_rms = lax.rsqrt(squares / model_width + EPSILON)
    qkv = (inv_rms[:, None] * merged).astype(jnp.bfloat16)
    out_grad = out_sum.astype(jnp.bfloat16)
    query_flat = qkv[:, : QH * HD]
    keys_own = qkv[:, QH * HD : QH * HD + HD]
    values_own = qkv[:, QH * HD + HD : qkv_cols]
    keys_all, values_all = (
        lax.all_gather(keys_own, "ctx", axis=0, tiled=True),
        lax.all_gather(values_own, "ctx", axis=0, tiled=True),
    )
    row_start = ctx_rank * row_count
    query_heads = query_flat.reshape(row_count, QH, HD)
    out_heads = out_grad.reshape(row_count, QH, HD)
    own_pos = lax.dynamic_slice_in_dim(positions, row_start, row_count)
    own_doc = lax.dynamic_slice_in_dim(documents, row_start, row_count)
    visible_mask = visible(own_pos, own_doc, positions, documents)
    scores = (
        jnp.einsum("qhc,kc->hqk", query_heads, keys_all, preferred_element_type=jnp.float32)
        * score_scale
    )
    attn_probs = softmax_rows(scores, visible_mask[None])
    probs_low = attn_probs.astype(jnp.bfloat16)
    grad_prob = jnp.einsum("qhc,kc->hqk", out_heads, values_all, preferred_element_type=jnp.float32)
    delta_row = jnp.sum(attn_probs * grad_prob, axis=-1, keepdims=True)
    grad_score = (attn_probs * (grad_prob - delta_row) * score_scale).astype(jnp.bfloat16)
    grad_query = jnp.einsum("hqk,kc->qhc", grad_score, keys_all, preferred_element_type=jnp.float32)
    grad_query = grad_query.reshape(row_count, QH * HD)
    key_terms = jnp.einsum(
        "hqk,qhc->kc", grad_score, query_heads, preferred_element_type=jnp.float32
    )
    value_terms = jnp.einsum(
        "hqk,qhc->kc", probs_low, out_heads, preferred_element_type=jnp.float32
    )
    grad_key, grad_value = (
        lax.psum_scatter(key_terms, "ctx", scatter_dimension=0, tiled=True),
        lax.psum_scatter(value_terms, "ctx", scatter_dimension=0, tiled=True),
    )
    grad_qkv = jnp.concatenate([grad_query, grad_key, grad_value], axis=1).astype(jnp.bfloat16)
    grad_scale = jnp.sum(grad_qkv.astype(jnp.float32) * merged, axis=1)
    back_term = jnp.einsum(
        "rc,dc->rd", grad_qkv, weight[:, :qkv_cols], preferred_element_type=jnp.float32
    )
    result = incoming.astype(jnp.float32) + inv_rms[:, None] * back_term
    result = result - (inv_rms**3 * grad_scale / model_width)[:, None] * stash_f
    return result.astype(jnp.bfloat16)


def body(fwd_acts, back_grads, stashed, layer_weights, span_order, fwd_docs, back_docs):
    sections = lax.axis_size("pipe")
    section_index = lax.axis_index("pipe")
    ctx_rank = lax.axis_index("ctx")
    row_count = fwd_acts.shape[1]
    span_len = row_count // SPANS
    model_width = fwd_acts.shape[2] * lax.axis_size("tp")
    tick_count = stashed.shape[1]
    offsets = jnp.arange(span_len, dtype=jnp.int32)
    positions = (span_order[:, None] * span_len + offsets[None, :]).reshape(-1)
    gathered = lax.all_gather(layer_weights, "ctx", axis=3, tiled=True)[:, 0]
    fwd_state = fwd_acts[0]
    back_state = back_grads[0]
    for tick_index in range(tick_count):
        fwd_slot = (section_index - tick_index) % sections
        fwd_half = jnp.where(section_index < tick_index, 1, 0)
        fwd_weight = lax.dynamic_index_in_dim(gathered, fwd_half, 0, keepdims=False)
        fwd_documents = seq_documents(fwd_docs, fwd_slot, span_order, span_len)
        fwd_state = forward_layer(
            fwd_state, fwd_weight, positions, fwd_documents, ctx_rank, model_width
        )
        fwd_state = from_behind(fwd_state, "pipe", 1)
        back_slot = (section_index + tick_index) % sections
        back_half = jnp.where(section_index + tick_index < sections, 1, 0)
        back_weight = lax.dynamic_index_in_dim(gathered, back_half, 0, keepdims=False)
        back_documents = seq_documents(back_docs, back_slot, span_order, span_len)
        back_state = backward_layer(
            stashed[0, tick_index],
            back_state,
            back_weight,
            positions,
            back_documents,
            ctx_rank,
            model_width,
        )
        back_state = from_behind(back_state, "pipe", -1)
    return (fwd_state[None], back_state[None])


def solution(mesh):
    return jax.shard_map(
        body,
        mesh=mesh,
        in_specs=(
            P("pipe", "ctx", "tp"),
            P("pipe", "ctx", "tp"),
            P("pipe", None, "ctx", "tp"),
            P(None, "pipe", "tp", "ctx"),
            P(),
            P(),
            P(),
        ),
        out_specs=(P("pipe", "ctx", "tp"), P("pipe", "ctx", "tp")),
        check_vma=False,
    )
```

profile of v0, /device:TPU:0, one launch (start us, length us, event | category | flops | bytes accessed | tf_op | source)
XLA Modules:
  0.0 726.2 jit_solution(2499580592522703212)
XLA Ops:
  16.3 53.8 %all-gather.2.cloned.1.call-done = bf16[2,1,4096,2304]{3,2,1,0:T(8,128)(2,1)} async-done(((bf16[2,1,4096,1152]{3,2,1,0:T(8,128)(2,1)}), bf16[2,1,4096,2304]{3,2,1,0:T(8,128)(2,1)}) %all-gather.2.cloned.1.call-update) | async-done | bytes 37748752 | tf_op jit(solution)/shard_map/all_gather | solution.py:135
  70.1 73.6 %dynamic-slice_bitcast_fusion = (bf16[4096,2304]{1,0:T(8,128)(2,1)}, bf16[4096,2304]{1,0:T(8,128)(2,1)}, bf16[4096,2304]{1,0:T(8,128)(2,1)}, bf16[4096,2304]{1,0...) fusion(bf16[2,1,4096,2304]{3,2,1,0:T(8,128)(2,1)} %all-gather.2.cloned.1.call-done, ...), kind=kLoop, calls=%fused_computation.15 | loop fusion | bytes 226492448 | tf_op jit(solution)/shard_map/jit(dynamic_index_in_dim)/squeeze | solution.py:149
  143.7 7.8 %fusion.84 = f32[128,1280]{0,1:T(8,128)} fusion(bf16[4096,2304]{1,0:T(8,128)(2,1)} %get-tuple-element.30, bf16[1,128,4096]{2,1,0:T(8,128)(2,1)S(1)} %copy-done.3), kind=kOutput, calls=%fused_computation.75 | convolution fusion | flops 1342177280 | bytes 12189696 | tf_op jit(solution)/shard_map/dot_general | solution.py:41
  151.6 5.7 fusion.139
  157.4 41.3 %all-reduce.17 = (f32[128]{0:T(128)S(1)}, bf16[128,1024]{0,1:T(8,128)(2,1)}, f32[128]{0:T(128)S(1)}) all-reduce(f32[128]{0:T(128)S(1)} %fusion.87, f32[128,1024]{0,1:T(8,128)S(1)} %fusion.139, f32[128]{0:T(128)S(1)} %get-tuple-element.3), channel_id=1, replica_groups=mesh['pipe'=4,'ctx'=2,'tp'=4] {'tp'}, use_global_device_ids=true, to_apply=%region_1.2 | all-reduce | flops 131328 | bytes 788480 | tf_op jit(solution)/shard_map/psum | solution.py:43
  198.7 4.5 all-reduce.12.cloned.1.call-done
  206.2 2.3 all_gather.40
  209.1 2.4 convolution_convert_fusion.5
  211.5 6.5 fusion.72
  219.5 8.6 %fusion.75 = f32[128,1280]{0,1:T(8,128)} fusion(bf16[4096,2304]{1,0:T(8,128)(2,1)} %get-tuple-element.27, bf16[1,3,128,4096]{3,2,1,0:T(8,128)(2,1)} %param.9), kind=kOutput, calls=%fused_computation.72 | convolution fusion | flops 1342177280 | bytes 12189696 | tf_op jit(solution)/shard_map/dot_general | solution.py:74
  228.1 16.1 %collective-permute-done = bf16[128,4096]{1,0:T(8,128)(2,1)S(1)} collective-permute-done((bf16[128,4096]{1,0:T(8,128)(2,1)S(1)}, bf16[128,4096]{1,0:T(8,128)(2,1)S(1)}, u32[]{:S(2)}, u32[]{:S(2)}) %collective-permute-start) | collective-permute-done | bytes 1048608 | tf_op jit(solution)/shard_map/ppermute | solution.py:17
  245.2 2.4 fusion.11
  247.7 58.9 %all-reduce.16.cloned.1.call-done = (f32[128,1280]{1,0:T(8,128)}, f32[128,1280]{0,1:T(8,128)}) async-done(((f32[128,1280]{1,0:T(8,128)}, f32[128,1280]{0,1:T(8,128)}), (f32[128,1280]{1,0:T(8,128)}, f32[128,1280]{0,1:T(8,128)})) %all-reduce.16.cloned.1.call-update) | async-done | bytes 1310736 | tf_op jit(solution)/shard_map/psum | solution.py:43
  314.3 3.3 convolution_bitcast_fusion.8
  320.1 2.6 convolution_convert_fusion.2
  325.8 9.9 %reduce-scatter.9.cloned.1.call-done = f32[128,128]{0,1:T(8,128)} async-done(((f32[256,128]{0,1:T(8,128)}), f32[128,128]{0,1:T(8,128)}) %reduce-scatter.9.cloned.1.call-update) | async-done | bytes 65552 | tf_op jit(solution)/shard_map/reduce_scatter | solution.py:113
  337.9 8.0 %fusion.63 = bf16[128,4096]{1,0:T(8,128)(2,1)S(1)} fusion(bf16[4096,2304]{1,0:T(8,128)(2,1)} %get-tuple-element.27, bf16[1,128,4096]{2,1,0:T(8,128)(2,1)} %param.8, f32[128]{0:T(128)S(1)} %fusion.295, f32[128]{0:T(128)S(1)} %add_rsqrt_fusion.2, bf16[1,3,128,4096]{3,2,1,0:T(8,128)(2,1)S(1)} %copy-done.1, bf16[128,128]{0,1:T(8,128)(2,1)S(1)} %convert.35, ...), kind=kOutput, calls=%fused_computation.59 | convolution fusion | flops 1346830336 | bytes 13960192 | tf_op jit(solution)/shard_map/rc,dc->rd/dot_general | solution.py:117
  345.8 2.7 collective-permute-start.3
  348.5 7.8 %fusion.78 = f32[128,1280]{0,1:T(8,128)} fusion(bf16[4096,2304]{1,0:T(8,128)(2,1)} %get-tuple-element.26, bf16[1,3,128,4096]{3,2,1,0:T(8,128)(2,1)S(1)} %copy-done.1), kind=kOutput, calls=%fused_computation.73 | convolution fusion | flops 1342177280 | bytes 12189696 | tf_op jit(solution)/shard_map/dot_general | solution.py:74
  356.6 14.8 %collective-permute-done.3 = bf16[128,4096]{1,0:T(8,128)(2,1)S(1)} collective-permute-done((bf16[128,4096]{1,0:T(8,128)(2,1)S(1)}, bf16[128,4096]{1,0:T(8,128)(2,1)S(1)}, u32[]{:S(2)}, u32[]{:S(2)}) %collective-permute-start.3) | collective-permute-done | bytes 1048608 | tf_op jit(solution)/shard_map/ppermute | solution.py:17
  372.4 4.8 fusion.29
  377.1 31.3 %all-reduce.18 = (f32[128]{0:T(128)S(1)}, bf16[128,1024]{1,0:T(8,128)(2,1)}, f32[128]{0:T(128)S(1)}) all-reduce(f32[128]{0:T(128)S(1)} %fusion.88, f32[128,1024]{1,0:T(8,128)S(1)} %fusion.29, f32[128]{0:T(128)S(1)} %get-tuple-element.4), channel_id=1, replica_groups=mesh['pipe'=4,'ctx'=2,'tp'=4] {'tp'}, use_global_device_ids=true, to_apply=%region_6.7 | all-reduce | flops 131328 | bytes 788480 | tf_op jit(solution)/shard_map/psum | solution.py:43
  413.0 2.5 convolution_convert_fusion.4
  415.4 6.5 fusion.69
  421.9 2.6 collective-permute-start.1
  424.5 8.1 %fusion.81 = f32[128,1280]{0,1:T(8,128)} fusion(bf16[4096,2304]{1,0:T(8,128)(2,1)} %get-tuple-element.25, bf16[1,3,128,4096]{3,2,1,0:T(8,128)(2,1)} %param.9), kind=kOutput, calls=%fused_computation.74 | convolution fusion | flops 1342177280 | bytes 12189696 | tf_op jit(solution)/shard_map/dot_general | solution.py:74
  432.7 16.2 %collective-permute-done.1 = bf16[128,4096]{1,0:T(8,128)(2,1)S(1)} collective-permute-done((bf16[128,4096]{1,0:T(8,128)(2,1)S(1)}, bf16[128,4096]{1,0:T(8,128)(2,1)S(1)}, u32[]{:S(2)}, u32[]{:S(2)}) %collective-permute-start.1) | collective-permute-done | bytes 1048608 | tf_op jit(solution)/shard_map/ppermute | solution.py:17
  450.0 2.4 fusion.9
  452.5 80.2 %all-reduce.14.cloned.1.call-done = (f32[128,1280]{1,0:T(8,128)}, f32[128,1280]{0,1:T(8,128)}, f32[128,1280]{0,1:T(8,128)}) async-done(((f32[128,1280]{1,0:T(8,128)}, f32[128,1280]{0,1:T(8,128)}, f32[128,1280]{0,1:T(8,128)}), (f32[128,1280]{1,0:T(8,128)}, f32[128,1280]{0,1:T(8,128)}, f32[128,1280]{0,1:T(8,128)})) %all-reduce.14.cloned.1.call-update) | async-done | bytes 1966096 | tf_op jit(solution)/shard_map/psum | solution.py:43
  540.5 3.4 convolution_bitcast_fusion.6
  543.9 2.2 convolution_bitcast_fusion.5
  546.2 2.7 convolution_convert_fusion.1
  551.4 10.0 %reduce-scatter.13.cloned.1.call-done = f32[128,128]{0,1:T(8,128)} async-done(((f32[256,128]{0,1:T(8,128)}), f32[128,128]{0,1:T(8,128)}) %reduce-scatter.13.cloned.1.call-update) | async-done | bytes 65552 | tf_op jit(solution)/shard_map/reduce_scatter | solution.py:113
  563.6 8.1 %fusion.93 = bf16[128,4096]{1,0:T(8,128)(2,1)S(1)} fusion(bf16[128,4096]{1,0:T(8,128)(2,1)} %copy-done.20, f32[128]{0:T(128)S(1)} %fusion.294, bf16[4096,2304]{1,0:T(8,128)(2,1)} %get-tuple-element.26, f32[128]{0:T(128)S(1)} %add_rsqrt_fusion.1, bf16[1,3,128,4096]{3,2,1,0:T(8,128)(2,1)S(1)} %copy-done.2, bf16[128,128]{0,1:T(8,128)(2,1)S(1)} %convert.38, ...), kind=kOutput, calls=%fused_computation.82 | convolution fusion | flops 1346830336 | bytes 13960192 | tf_op jit(solution)/shard_map/rc,dc->rd/dot_general | solution.py:117
  571.6 2.7 collective-permute-start.4
  574.6 22.6 %collective-permute-done.4 = bf16[128,4096]{1,0:T(8,128)(2,1)S(1)} collective-permute-done((bf16[128,4096]{1,0:T(8,128)(2,1)S(1)}, bf16[128,4096]{1,0:T(8,128)(2,1)S(1)}, u32[]{:S(2)}, u32[]{:S(2)}) %collective-permute-start.4) | collective-permute-done | bytes 1048608 | tf_op jit(solution)/shard_map/ppermute | solution.py:17
  598.2 5.5 fusion.27
  603.7 31.9 %all-reduce.19 = (f32[128]{0:T(128)S(1)}, bf16[128,1024]{1,0:T(8,128)(2,1)}, f32[128]{0:T(128)S(1)}) all-reduce(f32[128]{0:T(128)S(1)} %fusion.89, f32[128,1024]{1,0:T(8,128)} %fusion.27, f32[128]{0:T(128)S(1)} %get-tuple-element.2), channel_id=1, replica_groups=mesh['pipe'=4,'ctx'=2,'tp'=4] {'tp'}, use_global_device_ids=true, to_apply=%region_11.12 | all-reduce | flops 131328 | bytes 788480 | tf_op jit(solution)/shard_map/psum | solution.py:43
  640.7 2.3 convolution_bitcast_fusion
  644.6 3.3 convolution_bitcast_fusion.4
  656.8 2.4 convolution_convert_fusion.3
  659.2 7.6 %fusion.66 = bf16[128,4096]{1,0:T(8,128)(2,1)} fusion(bf16[128,1024]{0,1:T(8,128)(2,1)} %bitcast.371, bf16[4096,2304]{1,0:T(8,128)(2,1)} %get-tuple-element.28, bf16[128,4096]{1,0:T(8,128)(2,1)} %copy-done.4), kind=kOutput, calls=%fused_computation.60 | convolution fusion | flops 1075314688 | bytes 10747904 | tf_op jit(solution)/shard_map/rc,dc->rd/dot_general | solution.py:63
  666.8 2.5 collective-permute-start.2
  669.2 2.7 convolution_convert_fusion
  674.9 7.9 %fusion.96 = bf16[128,4096]{1,0:T(8,128)(2,1)S(1)} fusion(bf16[128,4096]{1,0:T(8,128)(2,1)} %copy-done.21, f32[128]{0:T(128)S(1)} %fusion.293, bf16[4096,2304]{1,0:T(8,128)(2,1)} %get-tuple-element.25, f32[128]{0:T(128)S(1)} %add_rsqrt_fusion, bf16[1,3,128,4096]{3,2,1,0:T(8,128)(2,1)S(1)} %copy-done.2, bf16[128,128]{0,1:T(8,128)(2,1)S(1)} %convert.41, ...), kind=kOutput, calls=%fused_computation.85 | convolution fusion | flops 1346830336 | bytes 13960192 | tf_op jit(solution)/shard_map/rc,dc->rd/dot_general | solution.py:117
  683.8 10.6 %collective-permute-done.2 = bf16[128,4096]{1,0:T(8,128)(2,1)} collective-permute-done((bf16[128,4096]{1,0:T(8,128)(2,1)}, bf16[128,4096]{1,0:T(8,128)(2,1)}, u32[]{:S(2)}, u32[]{:S(2)}) %collective-permute-start.2) | collective-permute-done | bytes 1048608 | tf_op jit(solution)/shard_map/ppermute | solution.py:17
  694.4 21.3 %collective-permute-done.5 = bf16[128,4096]{1,0:T(8,128)(2,1)S(1)} collective-permute-done((bf16[128,4096]{1,0:T(8,128)(2,1)S(1)}, bf16[128,4096]{1,0:T(8,128)(2,1)S(1)}, u32[]{:S(2)}, u32[]{:S(2)}) %collective-permute-start.5) | collective-permute-done | bytes 1048608 | tf_op jit(solution)/shard_map/ppermute | solution.py:17
  715.6 2.3 copy.158
  (185 shorter events, 71.3 us)
Async XLA Ops:
  7.2 0.9 copy-start.17
  7.2 1.0 copy-start.22
  7.2 8.4 %copy-start = (bf16[1,3,128,4096]{3,2,1,0:T(8,128)(2,1)S(1)}, bf16[1,3,128,4096]{3,2,1,0:T(8,128)(2,1)}, u32[]{:S(2)}) copy-start(bf16[1,3,128,4096]{3,2,1,0:T(8,128)(2,1)} %param.9) | copy-start | bytes 9437188
  7.2 62.9 %all-gather.2.cloned.1.call-start = ((), (), s32[]{:S(2)}) async-start(), calls=%async_computation.6 | async-start | bytes 56623104 | tf_op jit(solution)/shard_map/all_gather | solution.py:135
  7.9 195.2 %all-reduce.12.cloned.1.call-start = ((), (), s32[]{:S(2)}) async-start(), calls=%async_computation.7 | async-start | bytes 1310720 | tf_op jit(solution)/shard_map/psum | solution.py:43
  16.3 127.4 %copy-start.3 = (bf16[1,128,4096]{2,1,0:T(8,128)(2,1)S(1)}, bf16[1,128,4096]{2,1,0:T(8,128)(2,1)}, u32[]{:S(2)}) copy-start(bf16[1,128,4096]{2,1,0:T(8,128)(2,1)} %param.7) | copy-start | bytes 3145732
  143.7 7.9 %copy-start.19 = (bf16[1,128,4096]{2,1,0:T(8,128)(2,1)S(1)}, bf16[1,128,4096]{2,1,0:T(8,128)(2,1)}, u32[]{:S(2)}) copy-start(bf16[1,128,4096]{2,1,0:T(8,128)(2,1)} %param.8) | copy-start | bytes 3145732
  151.5 155.1 %all-reduce.16.cloned.1.call-start = ((), (), s32[]{:S(2)}) async-start(), calls=%async_computation.15 | async-start | bytes 2621440 | tf_op jit(solution)/shard_map/psum | solution.py:43
  151.6 56.9 %copy-start.16 = (pred[128,256]{0,1:T(8,128)(4,1)S(1)}, pred[128,256]{0,1:T(8,128)(4,1)}, u32[]{:S(2)}) copy-start(pred[128,256]{0,1:T(8,128)(4,1)} %get-tuple-element.48) | copy-start | bytes 98308
  209.1 36.1 %slice-start.5 = ((s8[18874368]{0:T(1024)(128)(4,1)}), s8[2097152]{0:T(1024)(128)(4,1)S(1)}, s32[]{:S(2)}) async-start(s8[18874368]{0:T(1024)(128)(4,1)} %bitcast.351), calls=%async_computation.21 | async-start | bytes 4194304
  211.5 33.7 %slice-start.6 = ((s8[18874368]{0:T(1024)(128)(4,1)}), s8[4194304]{0:T(1024)(128)(4,1)S(1)}, s32[]{:S(2)}) async-start(s8[18874368]{0:T(1024)(128)(4,1)} %bitcast.351), calls=%async_computation.22 | async-start | bytes 8388608
  211.5 33.7 %slice-start.7 = ((s8[18874368]{0:T(1024)(128)(4,1)}), s8[4194304]{0:T(1024)(128)(4,1)S(1)}, s32[]{:S(2)}) async-start(s8[18874368]{0:T(1024)(128)(4,1)} %bitcast.351), calls=%async_computation.23 | async-start | bytes 8388608
  218.0 27.2 %slice-start.8 = ((s8[18874368]{0:T(1024)(128)(4,1)}), s8[4194304]{0:T(1024)(128)(4,1)S(1)}, s32[]{:S(2)}) async-start(s8[18874368]{0:T(1024)(128)(4,1)} %bitcast.351), calls=%async_computation.24 | async-start | bytes 8388608
  218.0 27.2 %slice-start.9 = ((s8[18874368]{0:T(1024)(128)(4,1)}), s8[4194304]{0:T(1024)(128)(4,1)S(1)}, s32[]{:S(2)}) async-start(s8[18874368]{0:T(1024)(128)(4,1)} %bitcast.351), calls=%async_computation.25 | async-start | bytes 8388608
  218.0 26.2 %collective-permute-start = (bf16[128,4096]{1,0:T(8,128)(2,1)S(1)}, bf16[128,4096]{1,0:T(8,128)(2,1)S(1)}, u32[]{:S(2)}, u32[]{:S(2)}) collective-permute-start(bf16[128,4096]{1,0:T(8,128)(2,1)S(1)} %fusion.72), channel_id=1, source_target_pairs={{24,0},{0,8},{8,16},{16,24},{25,1},{1,9},{9,17},{17,25},{26,2},{2,... | collective-permute-start | bytes 3145736 | tf_op jit(solution)/shard_map/ppermute | solution.py:17
  244.2 1.0 copy-start.6
  245.2 66.3 %copy-start.10 = (bf16[128,1024]{0,1:T(8,128)(2,1)S(1)}, bf16[128,1024]{0,1:T(8,128)(2,1)}, u32[]{:S(2)}) copy-start(bf16[128,1024]{0,1:T(8,128)(2,1)} %get-tuple-element.18) | copy-start | bytes 786436
  245.2 67.6 %copy-start.15 = (pred[128,256]{0,1:T(8,128)(4,1)S(1)}, pred[128,256]{0,1:T(8,128)(4,1)}, u32[]{:S(2)}) copy-start(pred[128,256]{0,1:T(8,128)(4,1)} %get-tuple-element.45) | copy-start | bytes 98308
  247.6 77.3 %reduce-scatter.7.cloned.1.call-start = ((), (), s32[]{:S(2)}) async-start(), calls=%async_computation.8 | async-start | bytes 196608 | tf_op jit(solution)/shard_map/reduce_scatter | solution.py:112
  312.8 25.1 %copy-start.1 = (bf16[1,3,128,4096]{3,2,1,0:T(8,128)(2,1)S(1)}, bf16[1,3,128,4096]{3,2,1,0:T(8,128)(2,1)}, u32[]{:S(2)}) copy-start(bf16[1,3,128,4096]{3,2,1,0:T(8,128)(2,1)} %param.9) | copy-start | bytes 9437188
  317.6 18.1 %reduce-scatter.9.cloned.1.call-start = ((), (), s32[]{:S(2)}) async-start(), calls=%async_computation.9 | async-start | bytes 196608 | tf_op jit(solution)/shard_map/reduce_scatter | solution.py:113
  319.9 212.8 %all-reduce.14.cloned.1.call-start = ((), (), s32[]{:S(2)}) async-start(), calls=%async_computation.14 | async-start | bytes 3932160 | tf_op jit(solution)/shard_map/psum | solution.py:43
  345.8 25.6 %collective-permute-start.3 = (bf16[128,4096]{1,0:T(8,128)(2,1)S(1)}, bf16[128,4096]{1,0:T(8,128)(2,1)S(1)}, u32[]{:S(2)}, u32[]{:S(2)}) collective-permute-start(bf16[128,4096]{1,0:T(8,128)(2,1)S(1)} %fusion.63), channel_id=1, source_target_pairs={{8,0},{16,8},{24,16},{0,24},{9,1},{17,9},{25,17},{1,25},{10,2},{18... | collective-permute-start | bytes 3145736 | tf_op jit(solution)/shard_map/ppermute | solution.py:17
  348.5 7.8 %copy-start.7 = (bf16[128,4096]{1,0:T(8,128)(2,1)S(1)}, bf16[128,4096]{1,0:T(8,128)(2,1)}, u32[]{:S(2)}) copy-start(bf16[128,4096]{1,0:T(8,128)(2,1)} %copy-done.6) | copy-start | bytes 3145732
  356.3 52.2 %copy-start.9 = (f32[128,1280]{1,0:T(8,128)S(1)}, f32[128,1280]{1,0:T(8,128)}, u32[]{:S(2)}) copy-start(f32[128,1280]{1,0:T(8,128)} %get-tuple-element.23) | copy-start | bytes 1966084
  356.3 56.1 %copy-start.14 = (pred[128,256]{0,1:T(8,128)(4,1)S(1)}, pred[128,256]{0,1:T(8,128)(4,1)}, u32[]{:S(2)}) copy-start(pred[128,256]{0,1:T(8,128)(4,1)} %get-tuple-element.47) | copy-start | bytes 98308
  356.6 58.8 %copy-start.8 = (bf16[128,4096]{1,0:T(8,128)(2,1)S(1)}, bf16[128,4096]{1,0:T(8,128)(2,1)}, u32[]{:S(2)}) copy-start(bf16[128,4096]{1,0:T(8,128)(2,1)} %copy-done.6) | copy-start | bytes 3145732
  371.4 1.0 copy-start.20
  412.9 37.0 %slice-start = ((s8[18874368]{0:T(1024)(128)(4,1)}), s8[2097152]{0:T(1024)(128)(4,1)S(1)}, s32[]{:S(2)}) async-start(s8[18874368]{0:T(1024)(128)(4,1)} %bitcast.349), calls=%async_computation.16 | async-start | bytes 4194304
  415.4 34.5 %slice-start.1 = ((s8[18874368]{0:T(1024)(128)(4,1)}), s8[4194304]{0:T(1024)(128)(4,1)S(1)}, s32[]{:S(2)}) async-start(s8[18874368]{0:T(1024)(128)(4,1)} %bitcast.349), calls=%async_computation.17 | async-start | bytes 8388608
  415.4 34.5 %slice-start.2 = ((s8[18874368]{0:T(1024)(128)(4,1)}), s8[4194304]{0:T(1024)(128)(4,1)S(1)}, s32[]{:S(2)}) async-start(s8[18874368]{0:T(1024)(128)(4,1)} %bitcast.349), calls=%async_computation.18 | async-start | bytes 8388608
  421.9 27.0 %collective-permute-start.1 = (bf16[128,4096]{1,0:T(8,128)(2,1)S(1)}, bf16[128,4096]{1,0:T(8,128)(2,1)S(1)}, u32[]{:S(2)}, u32[]{:S(2)}) collective-permute-start(bf16[128,4096]{1,0:T(8,128)(2,1)S(1)} %fusion.69), channel_id=1, source_target_pairs={{24,0},{0,8},{8,16},{16,24},{25,1},{1,9},{9,17},{17,25},{26,2},{2,... | collective-permute-start | bytes 3145736 | tf_op jit(solution)/shard_map/ppermute | solution.py:17
  424.5 25.4 %slice-start.3 = ((s8[18874368]{0:T(1024)(128)(4,1)}), s8[4194304]{0:T(1024)(128)(4,1)S(1)}, s32[]{:S(2)}) async-start(s8[18874368]{0:T(1024)(128)(4,1)} %bitcast.349), calls=%async_computation.19 | async-start | bytes 8388608
  424.5 25.4 %slice-start.4 = ((s8[18874368]{0:T(1024)(128)(4,1)}), s8[4194304]{0:T(1024)(128)(4,1)S(1)}, s32[]{:S(2)}) async-start(s8[18874368]{0:T(1024)(128)(4,1)} %bitcast.349), calls=%async_computation.20 | async-start | bytes 8388608
  448.9 1.0 copy-start.4
  449.9 87.6 %copy-start.11 = (bf16[128,1024]{1,0:T(8,128)(2,1)S(1)}, bf16[128,1024]{1,0:T(8,128)(2,1)}, u32[]{:S(2)}) copy-start(bf16[128,1024]{1,0:T(8,128)(2,1)} %get-tuple-element.15) | copy-start | bytes 786436
  450.0 88.9 %copy-start.13 = (pred[128,256]{0,1:T(8,128)(4,1)S(1)}, pred[128,256]{0,1:T(8,128)(4,1)}, u32[]{:S(2)}) copy-start(pred[128,256]{0,1:T(8,128)(4,1)} %get-tuple-element.44) | copy-start | bytes 98308
  452.4 98.1 %reduce-scatter.11.cloned.1.call-start = ((), (), s32[]{:S(2)}) async-start(), calls=%async_computation.10 | async-start | bytes 196608 | tf_op jit(solution)/shard_map/reduce_scatter | solution.py:112
  538.9 24.6 %copy-start.2 = (bf16[1,3,128,4096]{3,2,1,0:T(8,128)(2,1)S(1)}, bf16[1,3,128,4096]{3,2,1,0:T(8,128)(2,1)}, u32[]{:S(2)}) copy-start(bf16[1,3,128,4096]{3,2,1,0:T(8,128)(2,1)} %param.9) | copy-start | bytes 9437188
  543.8 17.6 %reduce-scatter.13.cloned.1.call-start = ((), (), s32[]{:S(2)}) async-start(), calls=%async_computation.11 | async-start | bytes 196608 | tf_op jit(solution)/shard_map/reduce_scatter | solution.py:113
  546.1 125.8 %reduce-scatter.15.cloned.1.call-start = ((), (), s32[]{:S(2)}) async-start(), calls=%async_computation.12 | async-start | bytes 196608 | tf_op jit(solution)/shard_map/reduce_scatter | solution.py:112
  563.5 10.8 %copy-start.5 = (bf16[128,4096]{1,0:T(8,128)(2,1)S(1)}, bf16[128,4096]{1,0:T(8,128)(2,1)}, u32[]{:S(2)}) copy-start(bf16[128,4096]{1,0:T(8,128)(2,1)} %copy-done.4) | copy-start | bytes 3145732
  571.6 25.6 %collective-permute-start.4 = (bf16[128,4096]{1,0:T(8,128)(2,1)S(1)}, bf16[128,4096]{1,0:T(8,128)(2,1)S(1)}, u32[]{:S(2)}, u32[]{:S(2)}) collective-permute-start(bf16[128,4096]{1,0:T(8,128)(2,1)S(1)} %fusion.93), channel_id=1, source_target_pairs={{8,0},{16,8},{24,16},{0,24},{9,1},{17,9},{25,17},{1,25},{10,2},{18... | collective-permute-start | bytes 3145736 | tf_op jit(solution)/shard_map/ppermute | solution.py:17
  574.6 68.4 %copy-start.12 = (pred[128,256]{0,1:T(8,128)(4,1)S(1)}, pred[128,256]{0,1:T(8,128)(4,1)}, u32[]{:S(2)}) copy-start(pred[128,256]{0,1:T(8,128)(4,1)} %get-tuple-element.43) | copy-start | bytes 98308
  597.2 1.0 copy-start.21
  647.9 24.9 %reduce-scatter.17.cloned.1.call-start = ((), (), s32[]{:S(2)}) async-start(), calls=%async_computation.13 | async-start | bytes 196608 | tf_op jit(solution)/shard_map/reduce_scatter | solution.py:113
  666.8 27.6 %collective-permute-start.2 = (bf16[128,4096]{1,0:T(8,128)(2,1)}, bf16[128,4096]{1,0:T(8,128)(2,1)}, u32[]{:S(2)}, u32[]{:S(2)}) collective-permute-start(bf16[128,4096]{1,0:T(8,128)(2,1)} %fusion.66), channel_id=1, source_target_pairs={{24,0},{0,8},{8,16},{16,24},{25,1},{1,9},{9,17},{17,25},{26,2},{2,... | collective-permute-start | bytes 3145736 | tf_op jit(solution)/shard_map/ppermute | solution.py:17
  682.9 32.8 %collective-permute-start.5 = (bf16[128,4096]{1,0:T(8,128)(2,1)S(1)}, bf16[128,4096]{1,0:T(8,128)(2,1)S(1)}, u32[]{:S(2)}, u32[]{:S(2)}) collective-permute-start(bf16[128,4096]{1,0:T(8,128)(2,1)S(1)} %fusion.96), channel_id=1, source_target_pairs={{8,0},{16,8},{24,16},{0,24},{9,1},{17,9},{25,17},{1,25},{10,2},{18... | collective-permute-start | bytes 3145736 | tf_op jit(solution)/shard_map/ppermute | solution.py:17
  (1 other events, 0.9 us)
Sparse Core Ops, SparseCore 0:
  9.6 60.4 all-gather.1
  151.7 51.4 all-reduce.11
  247.7 58.8 all-reduce.15
  317.7 7.1 reduce-scatter.6
  327.0 8.6 reduce-scatter.8
  452.5 80.1 all-reduce.13
  544.0 6.5 reduce-scatter.10
  552.7 8.6 reduce-scatter.12
  648.1 6.6 reduce-scatter.14
  656.8 8.6 reduce-scatter.16
where the time goes:
time: 734 us; the launch traced here: 726 us
  waiting for transfers between devices  324 us (44%)
  matrix products  142 us (19%)
  blocking collectives  128 us (17%)
  local copies, waits for them, and re-layouts  85.9 us (12%)
  other arithmetic  18.5 us (3%)
  between operations  15.2 us (2%)
  starting transfers between devices  13.4 us (2%)
    psum x3, waiting for transfers between devices, forward_layer(): merged, squares = lax.psum((partial_m, partial_sq), 'tp')  144 us
    psum x3, blocking collectives, forward_layer(): merged, squares = lax.psum((partial_m, partial_sq), 'tp')  105 us
    ppermute x6, waiting for transfers between devices, from_behind(): return lax.ppermute(block, axis, route)  102 us
    squeeze x1, local copies, waits for them, and re-layouts, body(): lax.dynamic_index_in_dim(gathered, back_half, 0, keepdims=False)  73.6 us
    all_gather x1, waiting for transfers between devices, body(): gathered = lax.all_gather(layer_weights, 'ctx', axis=3, tiled=True)[:, 0]  53.8 us
    dot_general x3, matrix products, backward_layer(): jnp.dot(stash_point, weight[:, :qkv_cols], preferred_element_type=jnp.flo...  24.6 us
    dot_general x3, matrix products, backward_layer(): jnp.einsum('rc,dc->rd', grad_qkv, weight[:, :qkv_cols], preferred_element...  24 us
    dot_general x3, matrix products, forward_layer(): jnp.einsum('rc,dc->rd', attended, weight[:, qkv_cols:], preferred_element...  20.6 us
  transfers between devices with their start and end apart: 16, of which 14 were waited for; matrix products, arithmetic and copies ran while one was open for 11% of the time, Pallas kernels for 0%

commit v1 on v0

--- a/solution.py
+++ b/solution.py
@@ -1,6 +1,10 @@
+import functools
+
 import jax
 import jax.numpy as jnp
 from jax import lax
+from jax.experimental import pallas as pl
+from jax.experimental.pallas import tpu as pltpu
 from jax.sharding import PartitionSpec as P
 
 HD = 128
@@ -122,7 +126,7 @@
     return result.astype(jnp.bfloat16)
 
 
-def body(fwd_acts, back_grads, stashed, layer_weights, span_order, fwd_docs, back_docs):
+def plain_body(fwd_acts, back_grads, stashed, layer_weights, span_order, fwd_docs, back_docs):
     sections = lax.axis_size("pipe")
     section_index = lax.axis_index("pipe")
     ctx_rank = lax.axis_index("ctx")
@@ -161,9 +165,395 @@
     return (fwd_state[None], back_state[None])
 
 
+QKV = QH * HD + 2 * HD
+OC = QH * HD
+WIDE = 256
+PARTIAL = jnp.float32
+MESH = pl.DeviceIdType.MESH
+TRANS_B = (((1,), (1,)), ((), ()))
+TRANS_A = (((0,), (0,)), ((), ()))
+
+
+def dot_nt(a, b):
+    return lax.dot_general(a, b, TRANS_B, preferred_element_type=jnp.float32)
+
+
+def dot_tn(a, b):
+    return lax.dot_general(a, b, TRANS_A, preferred_element_type=jnp.float32)
+
+
+def dot_nn(a, b):
+    return jnp.dot(a, b, preferred_element_type=jnp.float32)
+
+
+class Place:
+    def __init__(self, send_sem, recv_sem):
+        self.p, self.c, self.t = (lax.axis_index(a) for a in ("pipe", "ctx", "tp"))
+        self.n = lax.axis_size("tp")
+        self.send_sem, self.recv_sem = send_sem, recv_sem
+
+    def to(self, d):
+        return lax.rem(self.t + d, self.n)
+
+    def source(self, d):
+        return lax.rem(self.t + self.n - d, self.n)
+
+    def copy(self, src, dst, sem, c, t):
+        return pltpu.make_async_remote_copy(
+            src_ref=src,
+            dst_ref=dst,
+            send_sem=self.send_sem.at[sem],
+            recv_sem=self.recv_sem.at[sem],
+            device_id=(self.p, c, t),
+            device_id_type=MESH,
+        )
+
+    def partner(self, src, dst, sem):
+        return self.copy(src, dst, sem, 1 - self.c, self.t)
+
+    def barrier(self):
+        sem = pltpu.get_barrier_semaphore()
+        for d in range(self.n):
+            for other in (0, 1):
+                if d == 0 and other == 0:
+                    continue
+                c = self.c if other == 0 else 1 - self.c
+                pl.semaphore_signal(sem, inc=1, device_id=(self.p, c, self.to(d)), device_id_type=MESH)
+        pl.semaphore_wait(sem, 2 * self.n - 1)
+
+
+def row_squares(full, sq):
+    @pl.loop(0, full.shape[0] // 32)
+    def _(i):
+        rows = pl.ds(pl.multiple_of(i * 32, 32), 32)
+        x = full[rows, :].astype(jnp.float32)
+        sq[rows, :] = jnp.broadcast_to(jnp.sum(x * x, axis=1, keepdims=True), (32, HD))
+
+
+def project_cols(full, w, first, count, out):
+    @pl.loop(0, count // WIDE)
+    def _(i):
+        at = pl.multiple_of(i * WIDE, WIDE)
+        res = dot_nn(full[...], w[:, pl.ds(pl.multiple_of(first + at, HD), WIDE)])
+        out[:, pl.ds(at, WIDE)] = res.astype(out.dtype)
+
+
+def scatter_start(pc, part, landing, cols, base, rows):
+    copies = []
+    for d in range(1, pc.n):
+        to = pc.to(d)
+        mine = pl.ds(pl.multiple_of(to * rows, rows), rows)
+        cp = pc.copy(part.at[mine, pl.ds(0, cols)], landing.at[d - 1, :, pl.ds(0, cols)], base + d, pc.c, to)
+        cp.start()
+        copies.append(cp)
+    return copies
+
+
+def scatter_sum(pc, copies, part, landing, cols, rows):
+    total = part[pl.ds(pl.multiple_of(pc.t * rows, rows), rows), pl.ds(0, cols)].astype(jnp.float32)
+    for d, cp in enumerate(copies):
+        cp.wait_recv()
+        total = total + landing[d, :, pl.ds(0, cols)].astype(jnp.float32)
+    for cp in copies:
+        cp.wait_send()
+    return total
+
+
+def gather_start(pc, whole, base, rows, c, first=1):
+    mine = pl.ds(pl.multiple_of(pc.t * rows, rows), rows)
+    copies = []
+    for d in range(first, pc.n):
+        cp = pc.copy(whole.at[mine], whole.at[mine], base + d, c, pc.to(d))
+        cp.start()
+        copies.append(cp)
+    return copies
+
+
+def gather_wait(pc, whole, base, rows, first=1):
+    for d in range(first, pc.n):
+        there = pl.ds(pl.multiple_of(pc.source(d) * rows, rows), rows)
+        pc.copy(whole.at[there], whole.at[there], base + d, pc.c, pc.source(d)).wait_recv()
+
+
+def probabilities(q, k, seen):
+    scores = dot_nt(q, k) * (HD ** (-0.5))
+    masked = jnp.where(seen, scores, -jnp.inf)
+    top = jnp.max(masked, axis=-1, keepdims=True)
+    e = jnp.where(seen, jnp.exp(masked - top), 0.0)
+    return e / jnp.sum(e, axis=-1, keepdims=True)
+
+
+def qkv_rows(pc, width, full, w, part, landing, sq, sq_in, kv, m_ref, q_ref, base, rows):
+    row_squares(full, sq)
+    sq_copies = scatter_start(pc, sq, sq_in, HD, base, rows)
+    project_cols(full, w, 0, QKV, part)
+    copies = scatter_start(pc, part, landing, QKV, base + 4, rows)
+    squares = scatter_sum(pc, sq_copies, sq, sq_in, HD, rows)
+    m = scatter_sum(pc, copies, part, landing, QKV, rows)
+    r = lax.rsqrt(squares / width + EPSILON)
+    qkv = (r[:, :1] * m).astype(jnp.bfloat16)
+    if m_ref is not None:
+        m_ref[...] = m
+    q_ref[...] = qkv[:, :OC]
+    mine = pl.ds(pl.multiple_of(pc.t * rows, rows), rows)
+    kv[mine, :] = qkv[:, OC:]
+    kv_copies = gather_start(pc, kv, base + 8, rows, 0)
+    gather_wait(pc, kv, base + 8, rows)
+    for cp in kv_copies:
+        cp.wait_send()
+    return r
+
+
+PIECES = 4
+
+
+def hand_over(pc, stage, landed, out, base, make):
+    span = out.shape[1] // PIECES
+    copies = []
+    for piece in range(PIECES):
+        make(piece, span)
+        cols = pl.ds(piece * span, span)
+        cp = pc.partner(stage.at[:, cols], landed.at[:, cols], base + piece)
+        cp.start()
+        copies.append(cp)
+    for cp in copies:
+        cp.wait_send()
+
+
+def take_over(pc, stage, landed, out, base):
+    span = out.shape[1] // PIECES
+    for piece in range(PIECES):
+        cols = pl.ds(piece * span, span)
+        pc.partner(stage.at[:, cols], landed.at[:, cols], base + piece).wait_recv()
+        out[:, cols] = landed[:, cols]
+
+
+def fetch_weight(pc, w_hbm, w, half, sem):
+    local = pltpu.make_async_copy(w_hbm.at[half], w.at[:, pl.ds(0, w_hbm.shape[2])], sem)
+    local.start()
+    return local
+
+
+def values_weight(pc, w_hbm, w, half, sem):
+    return pc.partner(w_hbm.at[half, :, pl.ds(0, HD)], w.at[:, pl.ds(QKV - HD, HD)], sem)
+
+
+def forward_kernel(tick, width, seen_ref, h_ref, w_hbm, out_ref, w, full, part, landing, sq, sq_in,
+                   kv, q_ref, o_all, stage, landed, local_sem, send_sem, recv_sem):
+    pc = Place(send_sem, recv_sem)
+    own = h_ref.shape[0]
+    rows = 2 * own // pc.n
+    sections = lax.axis_size("pipe")
+    half = (sections + tick - 1 - pc.p) // sections
+    local = fetch_weight(pc, w_hbm, w, half, local_sem)
+    pc.barrier()
+    own_rows = pl.ds(pl.multiple_of(pc.c * own, own), own)
+    hop = pc.partner(h_ref, full.at[own_rows], 0)
+    hop.start()
+    extra = values_weight(pc, w_hbm, w, half, 1)
+
+    @pl.when(pc.c == 1)
+    def _():
+        extra.start()
+
+    full[own_rows, :] = h_ref[...]
+    other_rows = pl.ds(pl.multiple_of((1 - pc.c) * own, own), own)
+    pc.partner(h_ref, full.at[other_rows], 0).wait_recv()
+    local.wait()
+
+    @pl.when(pc.c == 0)
+    def _():
+        extra.wait_recv()
+        qkv_rows(pc, width, full, w, part, landing, sq, sq_in, kv, None, q_ref, 8, rows)
+        seen = seen_ref[...] > 0.0
+        mine = pl.ds(pl.multiple_of(pc.t * rows, rows), rows)
+        for h in range(QH):
+            cols = pl.ds(h * HD, HD)
+            p = probabilities(q_ref[:, cols], kv[:, pl.ds(0, HD)], seen).astype(jnp.bfloat16)
+            o_all[mine, cols] = dot_nn(p, kv[:, pl.ds(HD, HD)]).astype(jnp.bfloat16)
+        copies = gather_start(pc, o_all, 20, rows, 1, first=0)
+        for cp in copies:
+            cp.wait_send()
+        take_over(pc, stage, landed, out_ref, 24)
+
+    @pl.when(pc.c == 1)
+    def _():
+        extra.wait_send()
+        gather_wait(pc, o_all, 20, rows, first=0)
+
+        def make(piece, span):
+            @pl.loop(0, span // WIDE)
+            def _(i):
+                at = pl.multiple_of(piece * span + i * WIDE, WIDE)
+                cols = pl.ds(at, WIDE)
+                update = dot_nt(o_all[...], w[cols, pl.ds(HD, OC)])
+                res = (full[:, cols].astype(jnp.float32) + update).astype(jnp.bfloat16)
+                stage[:, cols] = res[:own]
+                out_ref[:, cols] = res[own:]
+
+        hand_over(pc, stage, landed, out_ref, 24, make)
+
+    hop.wait_send()
+
+
+def backward_kernel(tick, width, seen_ref, u_ref, g_ref, w_hbm, out_ref, w, full, gfull, part, landing,
+                    sq, sq_in, kv, q_ref, m_ref, go_ref, dkv, dkv_in, e_all, rc, stage, landed,
+                    local_sem, send_sem, recv_sem):
+    pc = Place(send_sem, recv_sem)
+    own = u_ref.shape[0]
+    rows = 2 * own // pc.n
+    sections = lax.axis_size("pipe")
+    half = (2 * sections - 1 - pc.p - tick) // sections
+    local = fetch_weight(pc, w_hbm, w, half, local_sem)
+    pc.barrier()
+    own_rows = pl.ds(pl.multiple_of(pc.c * own, own), own)
+    other_rows = pl.ds(pl.multiple_of((1 - pc.c) * own, own), own)
+    extra = values_weight(pc, w_hbm, w, half, 1)
+    uhop = pc.partner(u_ref, full.at[own_rows], 0)
+    ghop = pc.partner(g_ref, gfull.at[own_rows], 2)
+
+    @pl.when(pc.c == 1)
+    def _():
+        uhop.start()
+        extra.start()
+
+    ghop.start()
+    gfull[own_rows, :] = g_ref[...]
+    local.wait()
+
+    @pl.when(pc.c == 0)
+    def _():
+        full[own_rows, :] = u_ref[...]
+        pc.partner(u_ref, full.at[other_rows], 0).wait_recv()
+        extra.wait_recv()
+        r = qkv_rows(pc, width, full, w, part, landing, sq, sq_in, kv, m_ref, q_ref, 8, rows)
+        pc.partner(go_ref, go_ref, 3).wait_recv()
+        seen = seen_ref[...] > 0.0
+        mine = pl.ds(pl.multiple_of(pc.t * rows, rows), rows)
+        k, v = kv[:, pl.ds(0, HD)], kv[:, pl.ds(HD, HD)]
+        dr = jnp.zeros((rows, 1), jnp.float32)
+        dk = jnp.zeros((2 * own, HD), jnp.float32)
+        dv = jnp.zeros((2 * own, HD), jnp.float32)
+        for h in range(QH):
+            cols = pl.ds(h * HD, HD)
+            q, go = q_ref[:, cols], go_ref[:, cols]
+            p = probabilities(q, k, seen)
+            dp = dot_nt(go, v)
+            delta = jnp.sum(p * dp, axis=-1, keepdims=True)
+            ds = (p * (dp - delta) * (HD ** (-0.5))).astype(jnp.bfloat16)
+            dq = dot_nn(ds, k).astype(jnp.bfloat16)
+            e_all[mine, cols] = dq
+            dr = dr + jnp.sum(dq.astype(jnp.float32) * m_ref[:, cols], axis=1, keepdims=True)
+            dk = dk + dot_tn(ds, q)
+            dv = dv + dot_tn(p.astype(jnp.bfloat16), go)
+        dkv[:, pl.ds(0, HD)] = dk
+        dkv[:, pl.ds(HD, HD)] = dv
+        copies = scatter_start(pc, dkv, dkv_in, 2 * HD, 24, rows)
+        last = scatter_sum(pc, copies, dkv, dkv_in, 2 * HD, rows).astype(jnp.bfloat16)
+        e_all[mine, pl.ds(OC, 2 * HD)] = last
+        dr = dr + jnp.sum(last.astype(jnp.float32) * m_ref[:, pl.ds(OC, 2 * HD)], axis=1, keepdims=True)
+        rc[mine, pl.ds(0, HD)] = r
+        rc[mine, pl.ds(HD, HD)] = r * r * r * dr / width
+        copies = gather_start(pc, e_all, 28, rows, 0) + gather_start(pc, rc, 32, rows, 0)
+        gather_wait(pc, e_all, 28, rows)
+        gather_wait(pc, rc, 32, rows)
+        for cp in copies:
+            cp.wait_send()
+        pc.partner(g_ref, gfull.at[other_rows], 2).wait_recv()
+
+        def make(piece, span):
+            @pl.loop(0, span // WIDE)
+            def _(i):
+                at = pl.multiple_of(piece * span + i * WIDE, WIDE)
+                cols = pl.ds(at, WIDE)
+                back = dot_nt(e_all[...], w[cols, :])
+                res = gfull[:, cols].astype(jnp.float32) + rc[:, pl.ds(0, 1)] * back
+                res = res - rc[:, pl.ds(HD, 1)] * full[:, cols].astype(jnp.float32)
+                res = res.astype(jnp.bfloat16)
+                out_ref[:, cols] = res[:own]
+                stage[:, cols] = res[own:]
+
+        hand_over(pc, stage, landed, out_ref, 36, make)
+
+    @pl.when(pc.c == 1)
+    def _():
+        pc.partner(g_ref, gfull.at[other_rows], 2).wait_recv()
+        project_cols(gfull, w, HD, OC, part)
+        copies = scatter_start(pc, part, landing, OC, 20, rows)
+        go_ref[...] = scatter_sum(pc, copies, part, landing, OC, rows).astype(jnp.bfloat16)
+        give = pc.partner(go_ref, go_ref, 3)
+        give.start()
+        give.wait_send()
+        uhop.wait_send()
+        extra.wait_send()
+        take_over(pc, stage, landed, out_ref, 36)
+
+    ghop.wait_send()
+
+
+def call(kernel, collective_id, operands, specs, like, scratch, flops):
+    return pl.pallas_call(
+        kernel,
+        out_shape=jax.ShapeDtypeStruct(like.shape, like.dtype),
+        in_specs=specs,
+        out_specs=pl.BlockSpec(memory_space=pltpu.VMEM),
+        scratch_shapes=scratch + [pltpu.SemaphoreType.DMA, pltpu.SemaphoreType.DMA((40,)), pltpu.SemaphoreType.DMA((40,))],
+        compiler_params=pltpu.CompilerParams(
+            collective_id=collective_id, has_side_effects=True, vmem_limit_bytes=48 * 2**20
+        ),
+        cost_estimate=pl.CostEstimate(flops=flops, bytes_accessed=12 * 2**20, transcendentals=0),
+    )(*operands)
+
+
+def fused_body(fwd_acts, back_grads, stashed, layer_weights, span_order, fwd_docs, back_docs):
+    sections, n = lax.axis_size("pipe"), lax.axis_size("tp")
+    p, t = lax.axis_index("pipe"), lax.axis_index("tp")
+    own, model = fwd_acts.shape[1:]
+    seq = 2 * own
+    rows = seq // n
+    span = own // SPANS
+    width = model * n
+    ticks = stashed.shape[1]
+    offsets = jnp.arange(span, dtype=jnp.int32)
+    positions = (span_order[:, None] * span + offsets[None, :]).reshape(-1)
+    weights = layer_weights[:, 0]
+    bf, f32 = jnp.bfloat16, jnp.float32
+    vm = pltpu.VMEM
+    shared = [
+        vm((seq, QKV), PARTIAL), vm((n - 1, rows, QKV), PARTIAL), vm((seq, HD), f32),
+        vm((n - 1, rows, HD), f32), vm((seq, 2 * HD), bf), vm((rows, OC), bf),
+    ]
+    edge = [vm((own, model), bf), vm((own, model), bf)]
+    fwd_scratch = [vm((model, QKV), bf), vm((seq, model), bf)] + shared + [vm((seq, OC), bf)] + edge
+    back_scratch = [vm((model, QKV), bf), vm((seq, model), bf), vm((seq, model), bf)] + shared + [
+        vm((rows, QKV), f32), vm((rows, OC), bf), vm((seq, 2 * HD), f32), vm((n - 1, rows, 2 * HD), f32),
+        vm((seq, QKV), bf), vm((seq, 2 * HD), f32)] + edge
+    in_vmem = pl.BlockSpec(memory_space=pltpu.VMEM)
+    anywhere = pl.BlockSpec(memory_space=pl.ANY)
+
+    def seen(docs, slot):
+        documents = seq_documents(docs, slot, span_order, span)
+        my_pos = lax.dynamic_slice_in_dim(positions, t * rows, rows)
+        my_doc = lax.dynamic_slice_in_dim(documents, t * rows, rows)
+        return visible(my_pos, my_doc, positions, documents).astype(f32)
+
+    fwd, back = fwd_acts[0], back_grads[0]
+    for tick in range(ticks):
+        fwd_seen = seen(fwd_docs, (p - tick) % sections)
+        fwd = call(functools.partial(forward_kernel, tick, width), tick, (fwd_seen, fwd, weights),
+                   [in_vmem, in_vmem, anywhere], fwd, fwd_scratch, 3 * 10**10)
+        fwd = from_behind(fwd, "pipe", 1)
+        back_seen = seen(back_docs, (p + tick) % sections)
+        back = call(functools.partial(backward_kernel, tick, width), ticks + tick,
+                    (back_seen, stashed[0, tick], back, weights),
+                    [in_vmem, in_vmem, in_vmem, anywhere], back, back_scratch, 3 * 10**10)
+        back = from_behind(back, "pipe", -1)
+    return (fwd[None], back[None])
+
+
 def solution(mesh):
     return jax.shard_map(
-        body,
+        fused_body if mesh.shape["tp"] <= 4 else plain_body,
         mesh=mesh,
         in_specs=(
             P("pipe", "ctx", "tp"),

time: 734 us -> 405 us (0.55); the launches traced: 726 us -> 405 us
  Pallas kernels: 0 us -> 359 us
  waiting for transfers between devices: 324 us -> 26.1 us
  matrix products: 142 us -> 0 us
  blocking collectives: 128 us -> 0 us
  local copies, waits for them, and re-layouts: 85.9 us -> 9.96 us
  other arithmetic: 18.5 us -> 0.87 us
  between operations: 15.2 us -> 0.87 us
    pallas_call x0 -> x6, Pallas kernels: none -> 359 us  [call(): pl.pallas_call(kernel, out_shape=jax.ShapeDtypeStruct(like.shape, like.dt...]
    psum x3 -> x0, waiting for transfers between devices: 144 us -> none  [forward_layer(): merged, squares = lax.psum((partial_m, partial_sq), 'tp')]
    dot_general x30 -> x0, matrix products: 135 us -> none  [the longest x3 24.6 us: backward_layer(): jnp.dot(stash_point, weight[:, :qkv_cols], preferred_element_type=jnp.flo...]
    psum x3 -> x0, blocking collectives: 105 us -> none  [forward_layer(): merged, squares = lax.psum((partial_m, partial_sq), 'tp')]
    ppermute x6, waiting for transfers between devices: 102 us -> 26.1 us  [from_behind(): return lax.ppermute(block, axis, route)]
    squeeze x1, local copies, waits for them, and re-layouts: 73.6 us -> 2.29 us  [fused_body(): stashed[0, tick]]
    all_gather x1 -> x0, waiting for transfers between devices: 53.8 us -> none  [body(): gathered = lax.all_gather(layer_weights, 'ctx', axis=3, tiled=True)[:, 0]]
    reduce_scatter x6 -> x0, waiting for transfers between devices: 23.8 us -> none  [the longest x3 20 us: backward_layer(): lax.psum_scatter(value_terms, 'ctx', scatter_dimension=0, tiled=True)]
  transfers between devices with their start and end apart: 16 -> 6, of which waited for: 14 -> 1; matrix products, arithmetic and copies ran while one was open for 11% -> 0% of each run, Pallas kernels for 0% -> 71%
where the time goes in v1:
time: 405 us
  Pallas kernels  359 us (89%)
  waiting for transfers between devices  26.1 us (6%)
  local copies, waits for them, and re-layouts  9.96 us (2%)
  starting transfers between devices  8.55 us (2%)
    pallas_call x6, Pallas kernels, call(): pl.pallas_call(kernel, out_shape=jax.ShapeDtypeStruct(like.shape, like.dt...  359 us
    ppermute x6, waiting for transfers between devices, from_behind(): return lax.ppermute(block, axis, route)  26.1 us
    ppermute x6, starting transfers between devices, from_behind(): return lax.ppermute(block, axis, route)  8.55 us
  transfers between devices with their start and end apart: 6, of which 1 were waited for; matrix products, arithmetic and copies ran while one was open for 0% of the time, Pallas kernels for 71%

profile of v1, /device:TPU:0, one launch (start us, length us, event | category | flops | bytes accessed | tf_op | source)
XLA Modules:
  0.0 405.1 jit_solution(11672381377639885743)
XLA Ops:
  0.7 0.9 fusion.8
  1.6 0.1 reshape.66
  1.6 0.7 broadcast_multiply_fusion
  2.3 0.6 gather_fusion
  2.9 0.1 eq.97
  2.9 0.1 reshape.67
  3.0 0.6 gather_fusion.1
  3.6 0.1 eq.101
  3.7 0.1 dynamic_slice.47
  3.7 0.1 dynamic_slice.49
  3.8 0.1 reshape.68
  3.9 0.6 gather_fusion.2
  4.4 0.1 eq.105
  4.5 0.1 dynamic_slice.51
  4.6 0.1 reshape.69
  4.7 0.6 gather_fusion.3
  5.2 0.1 eq.109
  5.3 0.1 dynamic_slice.53
  5.4 0.1 reshape.70
  5.5 0.6 gather_fusion.4
  6.0 0.1 eq.113
  6.1 0.1 dynamic_slice.55
  6.2 0.1 reshape.71
  6.3 0.6 gather_fusion.5
  6.8 0.1 eq.117
  6.9 0.1 dynamic_slice.57
  7.0 0.1 iota_add_fusion
  7.0 0.1 add.88
  7.1 0.1 dynamic_slice.45
  7.2 2.3 slice_bitcast_fusion
  9.5 0.1 fusion.5
  9.7 0.0 copy-start.1
  9.7 72.3 %shard_map.89 = bf16[128,4096]{1,0:T(8,128)(2,1)S(1)} custom-call(f32[64,256]{1,0:T(8,128)S(1)} %get-tuple-element.11.seen_ref, bf16[128,4096]{1,0:T(8,128)(2,1)S(1)} %get-tuple-element.8.u_ref, bf16[128,4096]{1,0:T(8,128)(2,1)S(1)} %bitcast.11, bf16[2,4096,1152]{2,1,0:T(8,128)(2,1)} %bitcast.15), custom_call_target="tpu_custom_call" | custom-call | flops 30000001024 | bytes 12582912 | tf_op jit(solution)/shard_map/pallas_call | solution.py:495
  82.0 2.5 collective-permute-start.3
  84.5 48.2 %shard_map.86 = bf16[128,4096]{1,0:T(8,128)(2,1)S(1)} custom-call(f32[64,256]{1,0:T(8,128)S(1)} %get-tuple-element.14.seen_ref, bf16[128,4096]{1,0:T(8,128)(2,1)S(1)} %bitcast.12, bf16[2,4096,1152]{2,1,0:T(8,128)(2,1)} %bitcast.16), custom_call_target="tpu_custom_call" | custom-call | flops 30000001024 | bytes 12582912 | tf_op jit(solution)/shard_map/pallas_call | solution.py:495
  132.8 0.1 collective-permute-start
  132.8 70.9 %shard_map.90 = bf16[128,4096]{1,0:T(8,128)(2,1)S(1)} custom-call(f32[64,256]{1,0:T(8,128)S(1)} %get-tuple-element.12.seen_ref, bf16[128,4096]{1,0:T(8,128)(2,1)S(1)} %get-tuple-element.10.u_ref, bf16[128,4096]{1,0:T(8,128)(2,1)S(1)} %collective-permute-done.3.g_ref, bf16[2,4096,1152]{2,1,0:T(8,128)(2,1)} %bitcast.17), custom_call_target="tpu_custom_call" | custom-call | flops 30000001024 | bytes 12582912 | tf_op jit(solution)/shard_map/pallas_call | solution.py:495
  203.8 2.9 collective-permute-start.4
  206.7 48.2 %shard_map.87 = bf16[128,4096]{1,0:T(8,128)(2,1)S(1)} custom-call(f32[64,256]{1,0:T(8,128)S(1)} %get-tuple-element.15.seen_ref, bf16[128,4096]{1,0:T(8,128)(2,1)S(1)} %collective-permute-done.h_ref, bf16[2,4096,1152]{2,1,0:T(8,128)(2,1)} %bitcast.18), custom_call_target="tpu_custom_call" | custom-call | flops 30000001024 | bytes 12582912 | tf_op jit(solution)/shard_map/pallas_call | solution.py:495
  254.9 0.1 collective-permute-start.1
  255.0 0.0 collective-permute-done.4.g_ref
  255.0 70.9 %shard_map.91 = bf16[128,4096]{1,0:T(8,128)(2,1)S(1)} custom-call(f32[64,256]{1,0:T(8,128)S(1)} %get-tuple-element.13.seen_ref, bf16[128,4096]{1,0:T(8,128)(2,1)S(1)} %get-tuple-element.9.u_ref, bf16[128,4096]{1,0:T(8,128)(2,1)S(1)} %collective-permute-done.4.g_ref, bf16[2,4096,1152]{2,1,0:T(8,128)(2,1)} %bitcast.19), custom_call_target="tpu_custom_call" | custom-call | flops 30000001024 | bytes 12582912 | tf_op jit(solution)/shard_map/pallas_call | solution.py:495
  325.9 2.9 collective-permute-start.5
  328.8 48.2 %shard_map.88 = bf16[128,4096]{1,0:T(8,128)(2,1)S(1)} custom-call(f32[64,256]{1,0:T(8,128)S(1)} %get-tuple-element.16.seen_ref, bf16[128,4096]{1,0:T(8,128)(2,1)S(1)} %collective-permute-done.1.h_ref, bf16[2,4096,1152]{2,1,0:T(8,128)(2,1)} %bitcast.20), custom_call_target="tpu_custom_call" | custom-call | flops 30000001024 | bytes 12582912 | tf_op jit(solution)/shard_map/pallas_call | solution.py:495
  377.1 0.1 collective-permute-start.2
  377.1 26.1 %collective-permute-done.2 = bf16[128,4096]{1,0:T(8,128)(2,1)S(1)} collective-permute-done((bf16[128,4096]{1,0:T(8,128)(2,1)S(1)}, bf16[128,4096]{1,0:T(8,128)(2,1)S(1)}, u32[]{:S(2)}, u32[]{:S(2)}) %collective-permute-start.2) | collective-permute-done | bytes 1048608 | tf_op jit(solution)/shard_map/ppermute | solution.py:21
  403.2 1.0 copy.11
  404.2 1.0 copy.12
  (8 shorter events, 0.0 us)
Async XLA Ops:
  7.2 2.4 copy-start
  9.7 74.9 %copy-start.1 = (bf16[1,128,4096]{2,1,0:T(8,128)(2,1)S(1)}, bf16[1,128,4096]{2,1,0:T(8,128)(2,1)}, u32[]{:S(2)}) copy-start(bf16[1,128,4096]{2,1,0:T(8,128)(2,1)} %param.7) | copy-start | bytes 3145732
  82.0 50.8 %collective-permute-start.3 = (bf16[128,4096]{1,0:T(8,128)(2,1)S(1)}, bf16[128,4096]{1,0:T(8,128)(2,1)S(1)}, u32[]{:S(2)}, u32[]{:S(2)}) collective-permute-start(bf16[128,4096]{1,0:T(8,128)(2,1)S(1)} %shard_map.89), channel_id=1, source_target_pairs={{8,0},{16,8},{24,16},{0,24},{9,1},{17,9},{25,17},{1,25},{10,2},{18... | collective-permute-start | bytes 3145736 | tf_op jit(solution)/shard_map/ppermute | solution.py:21
  132.8 73.9 %collective-permute-start = (bf16[128,4096]{1,0:T(8,128)(2,1)S(1)}, bf16[128,4096]{1,0:T(8,128)(2,1)S(1)}, u32[]{:S(2)}, u32[]{:S(2)}) collective-permute-start(bf16[128,4096]{1,0:T(8,128)(2,1)S(1)} %shard_map.86), channel_id=1, source_target_pairs={{24,0},{0,8},{8,16},{16,24},{25,1},{1,9},{9,17},{17,25},{26,2},{2,... | collective-permute-start | bytes 3145736 | tf_op jit(solution)/shard_map/ppermute | solution.py:21
  203.8 51.2 %collective-permute-start.4 = (bf16[128,4096]{1,0:T(8,128)(2,1)S(1)}, bf16[128,4096]{1,0:T(8,128)(2,1)S(1)}, u32[]{:S(2)}, u32[]{:S(2)}) collective-permute-start(bf16[128,4096]{1,0:T(8,128)(2,1)S(1)} %shard_map.90), channel_id=1, source_target_pairs={{8,0},{16,8},{24,16},{0,24},{9,1},{17,9},{25,17},{1,25},{10,2},{18... | collective-permute-start | bytes 3145736 | tf_op jit(solution)/shard_map/ppermute | solution.py:21
  254.9 73.9 %collective-permute-start.1 = (bf16[128,4096]{1,0:T(8,128)(2,1)S(1)}, bf16[128,4096]{1,0:T(8,128)(2,1)S(1)}, u32[]{:S(2)}, u32[]{:S(2)}) collective-permute-start(bf16[128,4096]{1,0:T(8,128)(2,1)S(1)} %shard_map.87), channel_id=1, source_target_pairs={{24,0},{0,8},{8,16},{16,24},{25,1},{1,9},{9,17},{17,25},{26,2},{2,... | collective-permute-start | bytes 3145736 | tf_op jit(solution)/shard_map/ppermute | solution.py:21
  325.9 51.2 %collective-permute-start.5 = (bf16[128,4096]{1,0:T(8,128)(2,1)S(1)}, bf16[128,4096]{1,0:T(8,128)(2,1)S(1)}, u32[]{:S(2)}, u32[]{:S(2)}) collective-permute-start(bf16[128,4096]{1,0:T(8,128)(2,1)S(1)} %shard_map.91), channel_id=1, source_target_pairs={{8,0},{16,8},{24,16},{0,24},{9,1},{17,9},{25,17},{1,25},{10,2},{18... | collective-permute-start | bytes 3145736 | tf_op jit(solution)/shard_map/ppermute | solution.py:21
  377.1 26.1 %collective-permute-start.2 = (bf16[128,4096]{1,0:T(8,128)(2,1)S(1)}, bf16[128,4096]{1,0:T(8,128)(2,1)S(1)}, u32[]{:S(2)}, u32[]{:S(2)}) collective-permute-start(bf16[128,4096]{1,0:T(8,128)(2,1)S(1)} %shard_map.88), channel_id=1, source_target_pairs={{24,0},{0,8},{8,16},{16,24},{25,1},{1,9},{9,17},{17,25},{26,2},{2,... | collective-permute-start | bytes 3145736 | tf_op jit(solution)/shard_map/ppermute | solution.py:21

commit v2 on v1

--- a/solution.py
+++ b/solution.py
@@ -168,7 +168,9 @@
 QKV = QH * HD + 2 * HD
 OC = QH * HD
 WIDE = 256
-PARTIAL = jnp.float32
+DEPTHS = 4
+KV_BLOCK = OC // WIDE
+ORDER = (0, 1, KV_BLOCK, 2, 3)
 MESH = pl.DeviceIdType.MESH
 TRANS_B = (((1,), (1,)), ((), ()))
 TRANS_A = (((0,), (0,)), ((), ()))
@@ -230,12 +232,37 @@
         sq[rows, :] = jnp.broadcast_to(jnp.sum(x * x, axis=1, keepdims=True), (32, HD))
 
 
-def project_cols(full, w, first, count, out):
-    @pl.loop(0, count // WIDE)
+def project_block(pc, full, w, first, j, exact, part, landing, base, rows):
+    cols = pl.ds(j * WIDE, WIDE)
+    depth = full.shape[1] // DEPTHS
+    exact[:, cols] = dot_nn(full[:, pl.ds(0, depth)], w[pl.ds(0, depth), pl.ds(first + j * WIDE, WIDE)])
+
+    @pl.loop(1, DEPTHS)
     def _(i):
-        at = pl.multiple_of(i * WIDE, WIDE)
-        res = dot_nn(full[...], w[:, pl.ds(pl.multiple_of(first + at, HD), WIDE)])
-        out[:, pl.ds(at, WIDE)] = res.astype(out.dtype)
+        deep = pl.ds(pl.multiple_of(i * depth, depth), depth)
+        exact[:, cols] += dot_nn(full[:, deep], w[deep, pl.ds(first + j * WIDE, WIDE)])
+
+    if part is None:
+        part = exact
+    else:
+        part[:, cols] = exact[:, cols].astype(part.dtype)
+    copies = []
+    for d in range(1, pc.n):
+        to = pc.to(d)
+        mine = pl.ds(pl.multiple_of(to * rows, rows), rows)
+        cp = pc.copy(part.at[mine, cols], landing.at[d - 1, :, cols], base + 3 * j + d - 1, pc.c, to)
+        cp.start()
+        copies.append(cp)
+    return copies
+
+
+def block_sum(pc, copies, j, exact, landing, rows):
+    cols = pl.ds(j * WIDE, WIDE)
+    total = exact[pl.ds(pl.multiple_of(pc.t * rows, rows), rows), cols]
+    for d, cp in enumerate(copies):
+        cp.wait_recv()
+        total = total + landing[d, :, cols].astype(jnp.float32)
+    return total
 
 
 def scatter_start(pc, part, landing, cols, base, rows):
@@ -283,23 +310,30 @@
     return e / jnp.sum(e, axis=-1, keepdims=True)
 
 
-def qkv_rows(pc, width, full, w, part, landing, sq, sq_in, kv, m_ref, q_ref, base, rows):
-    row_squares(full, sq)
-    sq_copies = scatter_start(pc, sq, sq_in, HD, base, rows)
-    project_cols(full, w, 0, QKV, part)
-    copies = scatter_start(pc, part, landing, QKV, base + 4, rows)
+def qkv_rows(pc, width, full, w, ready, exact, landing, sq, sq_in, kv, m_ref, q_ref, rows):
+    copies = {}
+    for j in ORDER:
+        ready(j)
+        copies[j] = project_block(pc, full, w, 0, j, exact, None, landing, 40, rows)
+        if j == KV_BLOCK:
+            row_squares(full, sq)
+            sq_copies = scatter_start(pc, sq, sq_in, HD, 4, rows)
     squares = scatter_sum(pc, sq_copies, sq, sq_in, HD, rows)
-    m = scatter_sum(pc, copies, part, landing, QKV, rows)
     r = lax.rsqrt(squares / width + EPSILON)
-    qkv = (r[:, :1] * m).astype(jnp.bfloat16)
-    if m_ref is not None:
-        m_ref[...] = m
-    q_ref[...] = qkv[:, :OC]
     mine = pl.ds(pl.multiple_of(pc.t * rows, rows), rows)
-    kv[mine, :] = qkv[:, OC:]
-    kv_copies = gather_start(pc, kv, base + 8, rows, 0)
-    gather_wait(pc, kv, base + 8, rows)
-    for cp in kv_copies:
+    for j in (KV_BLOCK, 0, 1, 2, 3):
+        cols = pl.ds(j * WIDE, WIDE)
+        m = block_sum(pc, copies[j], j, exact, landing, rows)
+        if m_ref is not None:
+            m_ref[:, cols] = m
+        qkv = (r[:, :1] * m).astype(jnp.bfloat16)
+        if j == KV_BLOCK:
+            kv[mine, :] = qkv
+            kv_copies = gather_start(pc, kv, 8, rows, 0)
+        else:
+            q_ref[:, cols] = qkv
+    gather_wait(pc, kv, 8, rows)
+    for cp in kv_copies + [cp for j in ORDER for cp in copies[j]]:
         cp.wait_send()
     return r
 
@@ -329,16 +363,19 @@
 
 
 def fetch_weight(pc, w_hbm, w, half, sem):
-    local = pltpu.make_async_copy(w_hbm.at[half], w.at[:, pl.ds(0, w_hbm.shape[2])], sem)
-    local.start()
-    return local
+    copies = {}
+    for j in ORDER:
+        cols = pl.ds(j * WIDE, min(WIDE, w_hbm.shape[2] - j * WIDE))
+        copies[j] = pltpu.make_async_copy(w_hbm.at[half, :, cols], w.at[:, cols], sem.at[j])
+        copies[j].start()
+    return copies
 
 
 def values_weight(pc, w_hbm, w, half, sem):
     return pc.partner(w_hbm.at[half, :, pl.ds(0, HD)], w.at[:, pl.ds(QKV - HD, HD)], sem)
 
 
-def forward_kernel(tick, width, seen_ref, h_ref, w_hbm, out_ref, w, full, part, landing, sq, sq_in,
+def forward_kernel(tick, width, seen_ref, h_ref, w_hbm, out_ref, w, full, exact, landing, sq, sq_in,
                    kv, q_ref, o_all, stage, landed, local_sem, send_sem, recv_sem):
     pc = Place(send_sem, recv_sem)
     own = h_ref.shape[0]
@@ -359,12 +396,15 @@
     full[own_rows, :] = h_ref[...]
     other_rows = pl.ds(pl.multiple_of((1 - pc.c) * own, own), own)
     pc.partner(h_ref, full.at[other_rows], 0).wait_recv()
-    local.wait()
 
     @pl.when(pc.c == 0)
     def _():
-        extra.wait_recv()
-        qkv_rows(pc, width, full, w, part, landing, sq, sq_in, kv, None, q_ref, 8, rows)
+        def ready(j):
+            local[j].wait()
+            if j == KV_BLOCK:
+                extra.wait_recv()
+
+        qkv_rows(pc, width, full, w, ready, exact, landing, sq, sq_in, kv, None, q_ref, rows)
         seen = seen_ref[...] > 0.0
         mine = pl.ds(pl.multiple_of(pc.t * rows, rows), rows)
         for h in range(QH):
@@ -379,6 +419,8 @@
     @pl.when(pc.c == 1)
     def _():
         extra.wait_send()
+        for j in ORDER:
+            local[j].wait()
         gather_wait(pc, o_all, 20, rows, first=0)
 
         def make(piece, span):
@@ -396,7 +438,7 @@
     hop.wait_send()
 
 
-def backward_kernel(tick, width, seen_ref, u_ref, g_ref, w_hbm, out_ref, w, full, gfull, part, landing,
+def backward_kernel(tick, width, seen_ref, u_ref, g_ref, w_hbm, out_ref, w, full, gfull, exact, part, go_in, landing,
                     sq, sq_in, kv, q_ref, m_ref, go_ref, dkv, dkv_in, e_all, rc, stage, landed,
                     local_sem, send_sem, recv_sem):
     pc = Place(send_sem, recv_sem)
@@ -419,14 +461,18 @@
 
     ghop.start()
     gfull[own_rows, :] = g_ref[...]
-    local.wait()
 
     @pl.when(pc.c == 0)
     def _():
         full[own_rows, :] = u_ref[...]
         pc.partner(u_ref, full.at[other_rows], 0).wait_recv()
-        extra.wait_recv()
-        r = qkv_rows(pc, width, full, w, part, landing, sq, sq_in, kv, m_ref, q_ref, 8, rows)
+
+        def ready(j):
+            local[j].wait()
+            if j == KV_BLOCK:
+                extra.wait_recv()
+
+        r = qkv_rows(pc, width, full, w, ready, exact, landing, sq, sq_in, kv, m_ref, q_ref, rows)
         pc.partner(go_ref, go_ref, 3).wait_recv()
         seen = seen_ref[...] > 0.0
         mine = pl.ds(pl.multiple_of(pc.t * rows, rows), rows)
@@ -452,8 +498,8 @@
         last = scatter_sum(pc, copies, dkv, dkv_in, 2 * HD, rows).astype(jnp.bfloat16)
         e_all[mine, pl.ds(OC, 2 * HD)] = last
         dr = dr + jnp.sum(last.astype(jnp.float32) * m_ref[:, pl.ds(OC, 2 * HD)], axis=1, keepdims=True)
-        rc[mine, pl.ds(0, HD)] = r
-        rc[mine, pl.ds(HD, HD)] = r * r * r * dr / width
+        lane = lax.broadcasted_iota(jnp.int32, (rows, HD), 1)
+        rc[mine, :] = jnp.where(lane < HD // 2, r, r * r * r * dr / width)
         copies = gather_start(pc, e_all, 28, rows, 0) + gather_start(pc, rc, 32, rows, 0)
         gather_wait(pc, e_all, 28, rows)
         gather_wait(pc, rc, 32, rows)
@@ -468,7 +514,7 @@
                 cols = pl.ds(at, WIDE)
                 back = dot_nt(e_all[...], w[cols, :])
                 res = gfull[:, cols].astype(jnp.float32) + rc[:, pl.ds(0, 1)] * back
-                res = res - rc[:, pl.ds(HD, 1)] * full[:, cols].astype(jnp.float32)
+                res = res - rc[:, pl.ds(HD // 2, 1)] * full[:, cols].astype(jnp.float32)
                 res = res.astype(jnp.bfloat16)
                 out_ref[:, cols] = res[:own]
                 stage[:, cols] = res[own:]
@@ -478,9 +524,14 @@
     @pl.when(pc.c == 1)
     def _():
         pc.partner(g_ref, gfull.at[other_rows], 2).wait_recv()
-        project_cols(gfull, w, HD, OC, part)
-        copies = scatter_start(pc, part, landing, OC, 20, rows)
-        go_ref[...] = scatter_sum(pc, copies, part, landing, OC, rows).astype(jnp.bfloat16)
+        for j in ORDER:
+            local[j].wait()
+        copies = [project_block(pc, gfull, w, HD, j, exact, part, go_in, 60, rows) for j in range(KV_BLOCK)]
+        for j in range(KV_BLOCK):
+            go_ref[:, pl.ds(j * WIDE, WIDE)] = block_sum(pc, copies[j], j, exact, go_in, rows).astype(jnp.bfloat16)
+        for group in copies:
+            for cp in group:
+                cp.wait_send()
         give = pc.partner(go_ref, go_ref, 3)
         give.start()
         give.wait_send()
@@ -497,7 +548,7 @@
         out_shape=jax.ShapeDtypeStruct(like.shape, like.dtype),
         in_specs=specs,
         out_specs=pl.BlockSpec(memory_space=pltpu.VMEM),
-        scratch_shapes=scratch + [pltpu.SemaphoreType.DMA, pltpu.SemaphoreType.DMA((40,)), pltpu.SemaphoreType.DMA((40,))],
+        scratch_shapes=scratch + [pltpu.SemaphoreType.DMA((KV_BLOCK + 1,)), pltpu.SemaphoreType.DMA((72,)), pltpu.SemaphoreType.DMA((72,))],
         compiler_params=pltpu.CompilerParams(
             collective_id=collective_id, has_side_effects=True, vmem_limit_bytes=48 * 2**20
         ),
@@ -520,14 +571,15 @@
     bf, f32 = jnp.bfloat16, jnp.float32
     vm = pltpu.VMEM
     shared = [
-        vm((seq, QKV), PARTIAL), vm((n - 1, rows, QKV), PARTIAL), vm((seq, HD), f32),
+        vm((seq, QKV), f32), vm((n - 1, rows, QKV), f32), vm((seq, HD), f32),
         vm((n - 1, rows, HD), f32), vm((seq, 2 * HD), bf), vm((rows, OC), bf),
     ]
     edge = [vm((own, model), bf), vm((own, model), bf)]
     fwd_scratch = [vm((model, QKV), bf), vm((seq, model), bf)] + shared + [vm((seq, OC), bf)] + edge
-    back_scratch = [vm((model, QKV), bf), vm((seq, model), bf), vm((seq, model), bf)] + shared + [
+    back_scratch = [vm((model, QKV), bf), vm((seq, model), bf), vm((seq, model), bf), shared[0],
+                    vm((seq, OC), bf), vm((n - 1, rows, OC), bf)] + shared[1:] + [
         vm((rows, QKV), f32), vm((rows, OC), bf), vm((seq, 2 * HD), f32), vm((n - 1, rows, 2 * HD), f32),
-        vm((seq, QKV), bf), vm((seq, 2 * HD), f32)] + edge
+        vm((seq, QKV), bf), vm((seq, HD), f32)] + edge
     in_vmem = pl.BlockSpec(memory_space=pltpu.VMEM)
     anywhere = pl.BlockSpec(memory_space=pl.ANY)
 

time: 405 us -> 360 us (0.89)
  Pallas kernels: 359 us -> 313 us
    pallas_call x6, Pallas kernels: 359 us -> 313 us  [call(): pl.pallas_call(kernel, out_shape=jax.ShapeDtypeStruct(like.shape, like.dt...]
  transfers between devices with their start and end apart: 6 -> 6, of which waited for: 1 -> 1; matrix products, arithmetic and copies ran while one was open for 0% -> 0% of each run, Pallas kernels for 71% -> 70%
where the time goes in v2:
time: 360 us
  Pallas kernels  313 us (87%)
  waiting for transfers between devices  26.1 us (7%)
  local copies, waits for them, and re-layouts  9.96 us (3%)
  starting transfers between devices  8.61 us (2%)
    pallas_call x6, Pallas kernels, call(): pl.pallas_call(kernel, out_shape=jax.ShapeDtypeStruct(like.shape, like.dt...  313 us
    ppermute x6, waiting for transfers between devices, from_behind(): return lax.ppermute(block, axis, route)  26.1 us
    ppermute x6, starting transfers between devices, from_behind(): return lax.ppermute(block, axis, route)  8.61 us
  transfers between devices with their start and end apart: 6, of which 1 were waited for; matrix products, arithmetic and copies ran while one was open for 0% of the time, Pallas kernels for 70%

profile of v2, /device:TPU:0, one launch (start us, length us, event | category | flops | bytes accessed | tf_op | source)
XLA Modules:
  0.0 359.7 jit_solution(278600457460944594)
XLA Ops:
  0.7 0.9 fusion.8
  1.6 0.1 reshape.66
  1.6 0.7 broadcast_multiply_fusion
  2.3 0.6 gather_fusion
  2.9 0.1 eq.97
  2.9 0.1 reshape.67
  3.0 0.6 gather_fusion.1
  3.6 0.1 eq.101
  3.7 0.1 dynamic_slice.47
  3.7 0.1 dynamic_slice.49
  3.8 0.1 reshape.68
  3.9 0.6 gather_fusion.2
  4.4 0.1 eq.105
  4.5 0.1 dynamic_slice.51
  4.6 0.1 reshape.69
  4.7 0.6 gather_fusion.3
  5.2 0.1 eq.109
  5.3 0.1 dynamic_slice.53
  5.4 0.1 reshape.70
  5.5 0.6 gather_fusion.4
  6.0 0.1 eq.113
  6.1 0.1 dynamic_slice.55
  6.2 0.1 reshape.71
  6.3 0.6 gather_fusion.5
  6.8 0.1 eq.117
  6.9 0.1 dynamic_slice.57
  7.0 0.1 iota_add_fusion
  7.0 0.1 add.88
  7.1 0.1 dynamic_slice.45
  7.2 2.3 slice_bitcast_fusion
  9.5 0.1 fusion.5
  9.7 0.0 copy-start.1
  9.7 62.1 %shard_map.89 = bf16[128,4096]{1,0:T(8,128)(2,1)S(1)} custom-call(f32[64,256]{1,0:T(8,128)S(1)} %get-tuple-element.11.seen_ref, bf16[128,4096]{1,0:T(8,128)(2,1)S(1)} %get-tuple-element.8.u_ref, bf16[128,4096]{1,0:T(8,128)(2,1)S(1)} %bitcast.11, bf16[2,4096,1152]{2,1,0:T(8,128)(2,1)} %bitcast.15), custom_call_target="tpu_custom_call" | custom-call | flops 30000001024 | bytes 12582912 | tf_op jit(solution)/shard_map/pallas_call | solution.py:546
  71.7 2.6 collective-permute-start.3
  74.3 43.3 %shard_map.86 = bf16[128,4096]{1,0:T(8,128)(2,1)S(1)} custom-call(f32[64,256]{1,0:T(8,128)S(1)} %get-tuple-element.14.seen_ref, bf16[128,4096]{1,0:T(8,128)(2,1)S(1)} %bitcast.12, bf16[2,4096,1152]{2,1,0:T(8,128)(2,1)} %bitcast.16), custom_call_target="tpu_custom_call" | custom-call | flops 30000001024 | bytes 12582912 | tf_op jit(solution)/shard_map/pallas_call | solution.py:546
  117.7 0.1 collective-permute-start
  117.7 60.8 %shard_map.90 = bf16[128,4096]{1,0:T(8,128)(2,1)S(1)} custom-call(f32[64,256]{1,0:T(8,128)S(1)} %get-tuple-element.12.seen_ref, bf16[128,4096]{1,0:T(8,128)(2,1)S(1)} %get-tuple-element.10.u_ref, bf16[128,4096]{1,0:T(8,128)(2,1)S(1)} %collective-permute-done.3.g_ref, bf16[2,4096,1152]{2,1,0:T(8,128)(2,1)} %bitcast.17), custom_call_target="tpu_custom_call" | custom-call | flops 30000001024 | bytes 12582912 | tf_op jit(solution)/shard_map/pallas_call | solution.py:546
  178.5 3.0 collective-permute-start.4
  181.5 43.1 %shard_map.87 = bf16[128,4096]{1,0:T(8,128)(2,1)S(1)} custom-call(f32[64,256]{1,0:T(8,128)S(1)} %get-tuple-element.15.seen_ref, bf16[128,4096]{1,0:T(8,128)(2,1)S(1)} %collective-permute-done.h_ref, bf16[2,4096,1152]{2,1,0:T(8,128)(2,1)} %bitcast.18), custom_call_target="tpu_custom_call" | custom-call | flops 30000001024 | bytes 12582912 | tf_op jit(solution)/shard_map/pallas_call | solution.py:546
  224.6 0.1 collective-permute-start.1
  224.7 60.8 %shard_map.91 = bf16[128,4096]{1,0:T(8,128)(2,1)S(1)} custom-call(f32[64,256]{1,0:T(8,128)S(1)} %get-tuple-element.13.seen_ref, bf16[128,4096]{1,0:T(8,128)(2,1)S(1)} %get-tuple-element.9.u_ref, bf16[128,4096]{1,0:T(8,128)(2,1)S(1)} %collective-permute-done.4.g_ref, bf16[2,4096,1152]{2,1,0:T(8,128)(2,1)} %bitcast.19), custom_call_target="tpu_custom_call" | custom-call | flops 30000001024 | bytes 12582912 | tf_op jit(solution)/shard_map/pallas_call | solution.py:546
  285.6 2.9 collective-permute-start.5
  288.4 0.0 collective-permute-done.1.h_ref
  288.4 43.2 %shard_map.88 = bf16[128,4096]{1,0:T(8,128)(2,1)S(1)} custom-call(f32[64,256]{1,0:T(8,128)S(1)} %get-tuple-element.16.seen_ref, bf16[128,4096]{1,0:T(8,128)(2,1)S(1)} %collective-permute-done.1.h_ref, bf16[2,4096,1152]{2,1,0:T(8,128)(2,1)} %bitcast.20), custom_call_target="tpu_custom_call" | custom-call | flops 30000001024 | bytes 12582912 | tf_op jit(solution)/shard_map/pallas_call | solution.py:546
  331.6 0.1 collective-permute-start.2
  331.7 26.1 %collective-permute-done.2 = bf16[128,4096]{1,0:T(8,128)(2,1)S(1)} collective-permute-done((bf16[128,4096]{1,0:T(8,128)(2,1)S(1)}, bf16[128,4096]{1,0:T(8,128)(2,1)S(1)}, u32[]{:S(2)}, u32[]{:S(2)}) %collective-permute-start.2) | collective-permute-done | bytes 1048608 | tf_op jit(solution)/shard_map/ppermute | solution.py:21
  357.8 1.0 copy.11
  358.7 1.0 copy.12
  (8 shorter events, 0.0 us)
Async XLA Ops:
  7.2 2.4 copy-start
  9.7 64.7 %copy-start.1 = (bf16[1,128,4096]{2,1,0:T(8,128)(2,1)S(1)}, bf16[1,128,4096]{2,1,0:T(8,128)(2,1)}, u32[]{:S(2)}) copy-start(bf16[1,128,4096]{2,1,0:T(8,128)(2,1)} %param.7) | copy-start | bytes 3145732
  71.7 46.0 %collective-permute-start.3 = (bf16[128,4096]{1,0:T(8,128)(2,1)S(1)}, bf16[128,4096]{1,0:T(8,128)(2,1)S(1)}, u32[]{:S(2)}, u32[]{:S(2)}) collective-permute-start(bf16[128,4096]{1,0:T(8,128)(2,1)S(1)} %shard_map.89), channel_id=1, source_target_pairs={{8,0},{16,8},{24,16},{0,24},{9,1},{17,9},{25,17},{1,25},{10,2},{18... | collective-permute-start | bytes 3145736 | tf_op jit(solution)/shard_map/ppermute | solution.py:21
  117.7 63.8 %collective-permute-start = (bf16[128,4096]{1,0:T(8,128)(2,1)S(1)}, bf16[128,4096]{1,0:T(8,128)(2,1)S(1)}, u32[]{:S(2)}, u32[]{:S(2)}) collective-permute-start(bf16[128,4096]{1,0:T(8,128)(2,1)S(1)} %shard_map.86), channel_id=1, source_target_pairs={{24,0},{0,8},{8,16},{16,24},{25,1},{1,9},{9,17},{17,25},{26,2},{2,... | collective-permute-start | bytes 3145736 | tf_op jit(solution)/shard_map/ppermute | solution.py:21
  178.5 46.2 %collective-permute-start.4 = (bf16[128,4096]{1,0:T(8,128)(2,1)S(1)}, bf16[128,4096]{1,0:T(8,128)(2,1)S(1)}, u32[]{:S(2)}, u32[]{:S(2)}) collective-permute-start(bf16[128,4096]{1,0:T(8,128)(2,1)S(1)} %shard_map.90), channel_id=1, source_target_pairs={{8,0},{16,8},{24,16},{0,24},{9,1},{17,9},{25,17},{1,25},{10,2},{18... | collective-permute-start | bytes 3145736 | tf_op jit(solution)/shard_map/ppermute | solution.py:21
  224.6 63.8 %collective-permute-start.1 = (bf16[128,4096]{1,0:T(8,128)(2,1)S(1)}, bf16[128,4096]{1,0:T(8,128)(2,1)S(1)}, u32[]{:S(2)}, u32[]{:S(2)}) collective-permute-start(bf16[128,4096]{1,0:T(8,128)(2,1)S(1)} %shard_map.87), channel_id=1, source_target_pairs={{24,0},{0,8},{8,16},{16,24},{25,1},{1,9},{9,17},{17,25},{26,2},{2,... | collective-permute-start | bytes 3145736 | tf_op jit(solution)/shard_map/ppermute | solution.py:21
  285.6 46.1 %collective-permute-start.5 = (bf16[128,4096]{1,0:T(8,128)(2,1)S(1)}, bf16[128,4096]{1,0:T(8,128)(2,1)S(1)}, u32[]{:S(2)}, u32[]{:S(2)}) collective-permute-start(bf16[128,4096]{1,0:T(8,128)(2,1)S(1)} %shard_map.91), channel_id=1, source_target_pairs={{8,0},{16,8},{24,16},{0,24},{9,1},{17,9},{25,17},{1,25},{10,2},{18... | collective-permute-start | bytes 3145736 | tf_op jit(solution)/shard_map/ppermute | solution.py:21
  331.6 26.1 %collective-permute-start.2 = (bf16[128,4096]{1,0:T(8,128)(2,1)S(1)}, bf16[128,4096]{1,0:T(8,128)(2,1)S(1)}, u32[]{:S(2)}, u32[]{:S(2)}) collective-permute-start(bf16[128,4096]{1,0:T(8,128)(2,1)S(1)} %shard_map.88), channel_id=1, source_target_pairs={{24,0},{0,8},{8,16},{16,24},{25,1},{1,9},{9,17},{17,25},{26,2},{2,... | collective-permute-start | bytes 3145736 | tf_op jit(solution)/shard_map/ppermute | solution.py:21
